TPU v7x, 32 devices: a whole 2x2x4 slice. The times are simulated.
32 devices in a mesh: dp: 8 (over z, y), mp: 4 (over x, core).
Axes of the slice: x: 2, y: 2, z: 4, core: 2. Of those that a mesh axis runs over, the one named last changes fastest.
Arguments:
- frames: bfloat16 [4, 4608, 768], P(None, ('dp', 'mp')), may hold values from -6 to 6
- clip_ids: int32 [4, 4608], replicated, may hold values from 0 to 5, never falling along the last dimension, each value on 1 to 1500 neighbouring positions
- w_qkv: bfloat16 [768, 3, 768], P('dp', None, 'mp'), may hold values from -0.21875 to 0.21875
- b_qv: bfloat16 [2, 4, 192], P(None, 'mp', 'dp'), may hold values from -3 to 3
- w_out: bfloat16 [768, 768], P('mp', 'dp'), may hold values from -2.5 to 2.5
- w_up: bfloat16 [768, 3072], P('dp', 'mp'), may hold values from -0.21875 to 0.21875
- b_up: bfloat16 [4, 768], P('mp', 'dp'), may hold values from -3 to 3
- w_down: bfloat16 [3072, 768], P('mp', 'dp'), may hold values from -0.109375 to 0.109375
- gains: bfloat16 [2, 768], P(None, ('dp', 'mp')), may hold values from 0.099609375 to 1.8984375
- biases: bfloat16 [4, 768], P(None, ('dp', 'mp')), may hold values from -3 to 3
- cotangent: bfloat16 [4, 4608, 768], P(None, ('dp', 'mp')), may hold values from -6 to 6
Outputs:
- output: bfloat16 [4, 4608, 768], P(None, ('dp', 'mp'))
- frames_grad: bfloat16 [4, 4608, 768], P(None, ('dp', 'mp'))
- grad_qkv: float32 [768, 3, 768], P('dp', None, 'mp')
- grad_bqv: float32 [2, 4, 192], P(None, 'mp', 'dp')
- grad_out: float32 [768, 768], P('mp', 'dp')
- grad_up: float32 [768, 3072], P('dp', 'mp')
- grad_bup: float32 [4, 768], P('mp', 'dp')
- grad_down: float32 [3072, 768], P('mp', 'dp')
- grad_gains: float32 [2, 768], P(None, ('dp', 'mp'))
- grad_biases: float32 [4, 768], P(None, ('dp', 'mp'))
Inputs may be any that keep to these rules, and one draw needn't show every extreme that they name: `clip_ids`: in each micro-batch the clip ids never fall along the frames; each clip is a run of 1 to 1500 frames, and one clip of each micro-batch has exactly 1500.
All inputs are finite; a program needn't handle non-finite values.
Results may differ from a plain program's by a relative error of at most 0.017.
Values may be sent and summed in bfloat16 or wider, within the bound.
No kernel may reach another device: no remote copies, remote signals or barrier semaphores. Data moves between devices by JAX's collectives and lax.ppermute only.
A program may use at most 192 MiB of HBM per device.

v0:
```python
import jax
import jax.numpy as jnp
from jax import lax
from jax.sharding import PartitionSpec as P

D = 768
HD = 64
CLIP = 1500
epsilon = 1e-05
masked_score = -1e30


def passed_along(array, axis, by):
    peers = lax.axis_size(axis)
    pairs = [(i, i + by) for i in range(peers) if 0 <= i + by < peers]
    return lax.ppermute(array, axis, pairs)


def shortened(array):
    return jax.tree.map(lambda a: a.astype(jnp.bfloat16) if a.dtype == jnp.float32 else a, array)


def normalize(values, gain_row, shift_row):
    middle = jnp.mean(values, axis=-1, keepdims=True)
    centred = values - middle
    spread_sq = jnp.mean(centred * centred, axis=-1, keepdims=True)
    return centred * lax.rsqrt(spread_sq + epsilon) * gain_row + shift_row


def gelu_exact(values):
    return jax.nn.gelu(values, approximate=False)


def fetch_weights(w_qkv, b_qv, w_out, w_up, b_up, w_down, gains, biases):
    gathered = (
        lax.all_gather(w_qkv, "dp", axis=0, tiled=True),
        lax.all_gather(b_qv, "dp", axis=2, tiled=True),
        lax.all_gather(w_out, "dp", axis=1, tiled=True),
        lax.all_gather(w_up, "dp", axis=0, tiled=True),
        lax.all_gather(b_up, "dp", axis=1, tiled=True),
        lax.all_gather(w_down, "dp", axis=1, tiled=True),
    )
    norm_rows = (
        lax.all_gather(gains, ("dp", "mp"), axis=1, tiled=True),
        lax.all_gather(biases, ("dp", "mp"), axis=1, tiled=True),
    )
    return (gathered, norm_rows)


def spread_rows(values):
    return lax.all_gather(values, "mp", axis=0, tiled=True)


def spread_grads(values):
    return lax.all_gather(values, "mp", axis=0, tiled=True)


def project_sum(left, weight, share_rows):

    def term(row_start, row_count):
        row_piece = lax.dynamic_slice_in_dim(left, row_start, row_count, 0)
        return jnp.dot(row_piece, weight, preferred_element_type=jnp.float32)

    return lax.psum_scatter(
        term(jnp.int32(0), share_rows * lax.axis_size("mp")).astype(jnp.bfloat16),
        "mp",
        scatter_dimension=0,
        tiled=True,
    ).astype(jnp.float32)


def project_back(left, weight, share_rows):

    def term(row_start, row_count):
        row_piece = lax.dynamic_slice_in_dim(left, row_start, row_count, 0)
        return lax.dot_general(
            row_piece, weight, (((1,), (1,)), ((), ())), preferred_element_type=jnp.float32
        )

    return lax.psum_scatter(
        term(jnp.int32(0), share_rows * lax.axis_size("mp")).astype(jnp.bfloat16),
        "mp",
        scatter_dimension=0,
        tiled=True,
    ).astype(jnp.float32)


def head_scores(query_head, key_head, same_clip):
    scores = jnp.einsum(
        "qd,kd->qk", query_head, key_head, preferred_element_type=jnp.float32
    ) * HD ** (-0.5)
    return jnp.where(same_clip, scores, masked_score)


def local(frames, clip_ids, w_qkv, b_qv, w_out, w_up, b_up, w_down, gains, biases, cotangent):
    share_rows = frames.shape[1]
    row_total = share_rows * lax.axis_size("mp")
    device = lax.axis_index("dp")
    frame_total = clip_ids.shape[1]
    width_local = w_qkv.shape[2]
    ff_local = w_up.shape[1]
    heads_local = width_local // HD
    reach_devs = (CLIP + row_total - 2) // row_total
    offsets = list(range(-reach_devs, reach_devs + 1))
    window = len(offsets) * row_total
    score_scale = HD ** (-0.5)
    key_place = (device - reach_devs) * row_total + jnp.arange(window, dtype=jnp.int32)
    key_valid = (key_place >= 0) & (key_place < frame_total)
    key_index = jnp.clip(key_place, 0, frame_total - 1)
    query_index = device * row_total + jnp.arange(row_total, dtype=jnp.int32)

    def forward_pass(inputs, clip_row, fetched):
        weights, norm_rows = fetched
        weight_qkv, bias_qv, weight_out, weight_up, bias_up, weight_down = weights
        gain_rows = norm_rows[0].astype(jnp.float32)
        bias_rows = norm_rows[1].astype(jnp.float32)
        key_clip = jnp.where(key_valid, jnp.take(clip_row, key_index), -1)
        query_clip = jnp.take(clip_row, query_index)
        same_clip = query_clip[:, None] == key_clip[None, :]
        resid_in = inputs.astype(jnp.float32)
        normed_one = normalize(resid_in, gain_rows[0], bias_rows[0]).astype(jnp.bfloat16)
        rows_one = spread_rows(normed_one)
        projected = jnp.dot(
            rows_one,
            weight_qkv.reshape(weight_qkv.shape[0], -1),
            preferred_element_type=jnp.float32,
        ).reshape(row_total, 3, width_local)
        bias_pair = bias_qv.reshape(2, width_local).astype(jnp.float32)
        projected = (
            projected + jnp.stack([bias_pair[0], jnp.zeros_like(bias_pair[0]), bias_pair[1]])[None]
        )
        projected = projected.astype(jnp.bfloat16)
        queries = projected[:, 0]
        key_value = projected[:, 1:]
        pieces = []
        for offset in offsets:
            if offset == 0:
                pieces.append(key_value)
            else:
                pieces.append(passed_along(key_value, "dp", -offset))
        near_rows = jnp.concatenate(pieces, axis=0)
        keys_near = near_rows[:, 0]
        values_near = near_rows[:, 1]
        head_outs = []
        log_totals = []
        for head_index in range(heads_local):
            columns = slice(head_index * HD, (head_index + 1) * HD)
            scores = head_scores(queries[:, columns], keys_near[:, columns], same_clip)
            top_score = jnp.max(scores, axis=-1, keepdims=True)
            log_total = top_score + jnp.log(
                jnp.sum(jnp.exp(scores - top_score), axis=-1, keepdims=True)
            )
            soft_weights = jnp.exp(scores - log_total).astype(jnp.bfloat16)
            head_outs.append(
                jnp.dot(soft_weights, values_near[:, columns], preferred_element_type=jnp.float32)
            )
            log_totals.append(log_total)
        attended = jnp.concatenate(head_outs, axis=-1).astype(jnp.bfloat16)
        mixed_rows = resid_in + project_sum(attended, weight_out, share_rows) + bias_rows[1]
        normed_two = normalize(mixed_rows, gain_rows[1], bias_rows[2]).astype(jnp.bfloat16)
        rows_two = spread_rows(normed_two)
        hidden = jnp.dot(rows_two, weight_up, preferred_element_type=jnp.float32) + bias_up.reshape(
            -1
        ).astype(jnp.float32)
        activated = gelu_exact(hidden).astype(jnp.bfloat16)
        result = mixed_rows + project_sum(activated, weight_down, share_rows) + bias_rows[3]
        kept_state = (
            resid_in,
            rows_one,
            queries,
            keys_near,
            values_near,
            same_clip,
            log_totals,
            attended,
            mixed_rows,
            rows_two,
            hidden,
            activated,
            query_clip,
            clip_row,
        )
        return (kept_state, result)

    def backward_pass(kept_state, cot_rows, fetched):
        weights, norm_rows = fetched
        weight_qkv, bias_qv, weight_out, weight_up, bias_up, weight_down = weights
        gain_rows = norm_rows[0].astype(jnp.float32)
        bias_rows = norm_rows[1].astype(jnp.float32)
        (
            resid_in,
            rows_one,
            queries,
            keys_near,
            values_near,
            same_clip,
            log_totals,
            attended,
            mixed_rows,
            rows_two,
            hidden,
            activated,
            query_clip,
            clip_row,
        ) = kept_state
        grad_result = cot_rows.astype(jnp.float32)
        rows_result = spread_grads(grad_result.astype(jnp.bfloat16))
        grad_wdown = jnp.einsum(
            "nf,nd->fd", activated, rows_result, preferred_element_type=jnp.float32
        )
        grad_act = lax.dot_general(
            rows_result, weight_down, (((1,), (1,)), ((), ())), preferred_element_type=jnp.float32
        )
        gelu_pull = jax.vjp(gelu_exact, hidden)[1]
        grad_hidden = gelu_pull(grad_act)[0].astype(jnp.bfloat16)
        grad_wup = jnp.einsum(
            "nd,nf->df", rows_two, grad_hidden, preferred_element_type=jnp.float32
        )
        grad_bup = jnp.sum(grad_hidden, axis=0, dtype=jnp.float32).reshape(1, ff_local)
        grad_two = project_back(grad_hidden, weight_up, share_rows)
        norm_pull_two = jax.vjp(normalize, mixed_rows, gain_rows[1], bias_rows[2])[1]
        grad_mix, grad_gain_two, grad_bias_two = norm_pull_two(grad_two)
        grad_mixed = grad_result + grad_mix
        rows_mixed = spread_grads(grad_mixed.astype(jnp.bfloat16))
        grad_wout = jnp.einsum(
            "nh,nd->hd", attended, rows_mixed, preferred_element_type=jnp.float32
        )
        grad_att = lax.dot_general(
            rows_mixed, weight_out, (((1,), (1,)), ((), ())), preferred_element_type=jnp.float32
        ).astype(jnp.bfloat16)
        query_grads = []
        key_grads = []
        value_grads = []
        row_deltas = []
        for head_index in range(heads_local):
            columns = slice(head_index * HD, (head_index + 1) * HD)
            query_head = queries[:, columns]
            key_head = keys_near[:, columns]
            grad_head = grad_att[:, columns]
            scores = head_scores(query_head, key_head, same_clip)
            soft_weights = jnp.exp(scores - log_totals[head_index])
            grad_soft = jnp.einsum(
                "qd,kd->qk", grad_head, values_near[:, columns], preferred_element_type=jnp.float32
            )
            row_delta = jnp.sum(grad_soft * soft_weights, axis=-1, keepdims=True)
            row_deltas.append(row_delta)
            grad_scores = (soft_weights * (grad_soft - row_delta)).astype(jnp.bfloat16)
            query_grads.append(
                jnp.dot(grad_scores, key_head, preferred_element_type=jnp.float32) * score_scale
            )
            key_grads.append(
                jnp.einsum("qk,qd->kd", grad_scores, query_head, preferred_element_type=jnp.float32)
                * score_scale
            )
            value_grads.append(
                jnp.einsum(
                    "qk,qd->kd",
                    soft_weights.astype(jnp.bfloat16),
                    grad_head,
                    preferred_element_type=jnp.float32,
                )
            )
        grad_queries = jnp.concatenate(query_grads, axis=-1)
        kv_total = jnp.zeros((row_total, 2, width_local), jnp.float32)
        stacked = jnp.stack(
            [jnp.concatenate(key_grads, axis=-1), jnp.concatenate(value_grads, axis=-1)], axis=1
        )
        for place_index, offset in enumerate(offsets):
            segment_grad = stacked[place_index * row_total : (place_index + 1) * row_total]
            if offset == 0:
                kv_total = kv_total + segment_grad
            else:
                kv_total = kv_total + passed_along(shortened(segment_grad), "dp", offset).astype(
                    segment_grad.dtype
                )
        grad_proj = jnp.concatenate([grad_queries[:, None], kv_total], axis=1).astype(jnp.bfloat16)
        grad_wqkv = jnp.einsum(
            "nd,nce->dce", rows_one, grad_proj, preferred_element_type=jnp.float32
        )
        grad_bqv = jnp.stack(
            [
                jnp.sum(grad_proj[:, 0], axis=0, dtype=jnp.float32),
                jnp.sum(grad_proj[:, 2], axis=0, dtype=jnp.float32),
            ]
        ).reshape(2, 1, width_local)
        grad_one = project_back(
            grad_proj.reshape(row_total, -1),
            weight_qkv.reshape(weight_qkv.shape[0], -1),
            share_rows,
        )
        norm_pull_one = jax.vjp(normalize, resid_in, gain_rows[0], bias_rows[0])[1]
        grad_in_norm, grad_gain_one, grad_bias_one = norm_pull_one(grad_one)
        grad_inputs = (grad_mixed + grad_in_norm).astype(jnp.bfloat16)
        grad_gain_rows = jnp.stack([grad_gain_one, grad_gain_two])
        grad_bias_rows = jnp.stack(
            [
                grad_bias_one,
                jnp.sum(grad_mixed, axis=0),
                grad_bias_two,
                jnp.sum(grad_result, axis=0),
            ]
        )
        grad_parts = (
            grad_wqkv,
            grad_bqv,
            grad_wout,
            grad_wup,
            grad_bup,
            grad_wdown,
            grad_gain_rows,
            grad_bias_rows,
        )
        return (grad_parts, grad_inputs)

    def step(totals, step_items):
        inputs, clip_row, cot_rows = step_items
        front_weights = fetch_weights(w_qkv, b_qv, w_out, w_up, b_up, w_down, gains, biases)
        kept_state, result = forward_pass(inputs, clip_row, front_weights)
        fenced = lax.optimization_barrier(
            (w_qkv, b_qv, w_out, w_up, b_up, w_down, gains, biases, result)
        )
        behind = fetch_weights(
            fenced[0], fenced[1], fenced[2], fenced[3], fenced[4], fenced[5], fenced[6], fenced[7]
        )
        grad_parts, grad_inputs = backward_pass(kept_state, cot_rows, behind)
        totals = tuple((running + grad_part for running, grad_part in zip(totals, grad_parts)))
        return (totals, (result.astype(jnp.bfloat16), grad_inputs))

    zeros_start = (
        jnp.zeros((D, 3, width_local), jnp.float32),
        jnp.zeros((2, 1, width_local), jnp.float32),
        jnp.zeros((width_local, D), jnp.float32),
        jnp.zeros((D, ff_local), jnp.float32),
        jnp.zeros((1, ff_local), jnp.float32),
        jnp.zeros((ff_local, D), jnp.float32),
        jnp.zeros((2, D), jnp.float32),
        jnp.zeros((4, D), jnp.float32),
    )
    totals, (output, frames_grad) = lax.scan(step, zeros_start, (frames, clip_ids, cotangent))
    owned = (
        lax.psum_scatter(totals[0], "dp", scatter_dimension=0, tiled=True),
        lax.psum_scatter(totals[1], "dp", scatter_dimension=2, tiled=True),
        lax.psum_scatter(totals[2], "dp", scatter_dimension=1, tiled=True),
        lax.psum_scatter(totals[3], "dp", scatter_dimension=0, tiled=True),
        lax.psum_scatter(totals[4], "dp", scatter_dimension=1, tiled=True),
        lax.psum_scatter(totals[5], "dp", scatter_dimension=1, tiled=True),
    )
    owned_norms = (
        lax.psum_scatter(totals[6], ("dp", "mp"), scatter_dimension=1, tiled=True),
        lax.psum_scatter(totals[7], ("dp", "mp"), scatter_dimension=1, tiled=True),
    )
    return (
        output,
        frames_grad,
        owned[0],
        owned[1],
        owned[2],
        owned[3],
        owned[4],
        owned[5],
        owned_norms[0],
        owned_norms[1],
    )


def solution(mesh):
    placed = (
        P(None, ("dp", "mp"), None),
        P(),
        P("dp", None, "mp"),
        P(None, "mp", "dp"),
        P("mp", "dp"),
        P("dp", "mp"),
        P("mp", "dp"),
        P("mp", "dp"),
        P(None, ("dp", "mp")),
        P(None, ("dp", "mp")),
        P(None, ("dp", "mp"), None),
    )
    return jax.shard_map(
        local,
        mesh=mesh,
        in_specs=placed,
        out_specs=(
            P(None, ("dp", "mp"), None),
            P(None, ("dp", "mp"), None),
            P("dp", None, "mp"),
            P(None, "mp", "dp"),
            P("mp", "dp"),
            P("dp", "mp"),
            P("mp", "dp"),
            P("mp", "dp"),
            P(None, ("dp", "mp")),
            P(None, ("dp", "mp")),
        ),
        check_vma=False,
    )
```

profile of v0, /device:TPU:0, one launch (start us, length us, event | category | flops | bytes accessed | tf_op | source)
XLA Modules:
  0.0 3567.8 jit_solution(23908522268389208)
XLA Ops:
  9.8 3200.0 %while.31 = (s32[]{:T(128)}, f32[768,3,192]{0,2,1:T(8,128)}, f32[2,1,192]{2,1,0:T(1,128)}, f32[192,768]{1,0:T(8,128)}, f32[768,768]{1,0:T(8,128)}, /*index=5*/f3...) while((s32[]{:T(128)}, f32[768,3,192]{0,2,1:T(8,128)}, ...), condition=%wide.region_31.32_spmd.clone.clone.clone, body=%wide.region_0.31_spmd.clone.clone.clone.sunk | while | flops 11638805504 | bytes 781726784 | solution.py:339
  12.4 43.5 %all-gather.21 = bf16[32,24,2]{1,2,0:T(2,128)(2,1)S(1)} all-gather(bf16[1,24,2]{1,2,0:T(2,128)(2,1)} %bitcast.337), channel_id=1, replica_groups=mesh['dp'=8,'mp'=4] {'dp','mp'}, dimensions={0}, use_global_device_ids=true | all-gather | bytes 3168 | tf_op jit(solution)/shard_map/while/body/eval_jaxpr/all_gather | solution.py:44
  56.1 37.0 %all-gather.20 = bf16[32,24,4]{1,2,0:T(4,128)(2,1)S(1)} all-gather(bf16[1,24,4]{1,2,0:T(4,128)(2,1)} %bitcast.340), channel_id=1, replica_groups=mesh['dp'=8,'mp'=4] {'dp','mp'}, dimensions={0}, use_global_device_ids=true | all-gather | bytes 6336 | tf_op jit(solution)/shard_map/while/body/eval_jaxpr/all_gather | solution.py:45
  136.7 37.0 %all_gather.99 = bf16[768,3,192]{2,1,0:T(4,128)(2,1)S(1)} all-gather(bf16[96,3,192]{2,1,0:T(4,128)(2,1)S(1)} %copy.86), channel_id=1, replica_groups=mesh['dp'=8,'mp'=4] {'dp'}, dimensions={0}, use_global_device_ids=true | all-gather | bytes 995328 | tf_op jit(solution)/shard_map/while/body/eval_jaxpr/all_gather | solution.py:36
  476.7 36.6 %all-gather.35.cloned.1.call-done = bf16[768,768]{1,0:T(8,128)(2,1)} async-done(((bf16[96,768]{1,0:T(8,128)(2,1)}), bf16[768,768]{1,0:T(8,128)(2,1)}) %all-gather.35.cloned.1.call-update) | async-done | bytes 1179664 | tf_op jit(solution)/shard_map/while/body/eval_jaxpr/all_gather | solution.py:39
  521.3 38.9 %all-gather.23 = bf16[32,24,2]{1,2,0:T(2,128)(2,1)S(1)} all-gather(bf16[1,24,2]{1,2,0:T(2,128)(2,1)S(1)} %bitcast.338), channel_id=1, replica_groups=mesh['dp'=8,'mp'=4] {'dp','mp'}, dimensions={0}, use_global_device_ids=true | all-gather | bytes 3168 | tf_op jit(solution)/shard_map/while/body/eval_jaxpr/all_gather | solution.py:44
  594.1 37.0 %all_gather.110 = bf16[768,3,192]{2,0,1:T(8,128)(2,1)} all-gather(bf16[96,3,192]{2,0,1:T(8,128)(2,1)S(1)} %copy-done.32), channel_id=1, replica_groups=mesh['dp'=8,'mp'=4] {'dp'}, dimensions={0}, use_global_device_ids=true | all-gather | bytes 995328 | tf_op jit(solution)/shard_map/while/body/eval_jaxpr/all_gather | solution.py:36
  769.8 35.0 reduce-scatter.33.cloned.1.call-done
  812.0 40.7 %all-gather.21 = bf16[32,24,2]{1,2,0:T(2,128)(2,1)S(1)} all-gather(bf16[1,24,2]{1,2,0:T(2,128)(2,1)} %bitcast.337), channel_id=1, replica_groups=mesh['dp'=8,'mp'=4] {'dp','mp'}, dimensions={0}, use_global_device_ids=true | all-gather | bytes 3168 | tf_op jit(solution)/shard_map/while/body/eval_jaxpr/all_gather | solution.py:44
  853.0 37.0 %all-gather.20 = bf16[32,24,4]{1,2,0:T(4,128)(2,1)S(1)} all-gather(bf16[1,24,4]{1,2,0:T(4,128)(2,1)} %bitcast.340), channel_id=1, replica_groups=mesh['dp'=8,'mp'=4] {'dp','mp'}, dimensions={0}, use_global_device_ids=true | all-gather | bytes 6336 | tf_op jit(solution)/shard_map/while/body/eval_jaxpr/all_gather | solution.py:45
  933.5 37.0 %all_gather.99 = bf16[768,3,192]{2,1,0:T(4,128)(2,1)S(1)} all-gather(bf16[96,3,192]{2,1,0:T(4,128)(2,1)S(1)} %copy.86), channel_id=1, replica_groups=mesh['dp'=8,'mp'=4] {'dp'}, dimensions={0}, use_global_device_ids=true | all-gather | bytes 995328 | tf_op jit(solution)/shard_map/while/body/eval_jaxpr/all_gather | solution.py:36
  1165.0 34.3 all-gather.31.cloned.1.call-done
  1273.7 36.4 %all-gather.35.cloned.1.call-done = bf16[768,768]{1,0:T(8,128)(2,1)} async-done(((bf16[96,768]{1,0:T(8,128)(2,1)}), bf16[768,768]{1,0:T(8,128)(2,1)}) %all-gather.35.cloned.1.call-update) | async-done | bytes 1179664 | tf_op jit(solution)/shard_map/while/body/eval_jaxpr/all_gather | solution.py:39
  1318.9 38.9 %all-gather.23 = bf16[32,24,2]{1,2,0:T(2,128)(2,1)S(1)} all-gather(bf16[1,24,2]{1,2,0:T(2,128)(2,1)S(1)} %bitcast.338), channel_id=1, replica_groups=mesh['dp'=8,'mp'=4] {'dp','mp'}, dimensions={0}, use_global_device_ids=true | all-gather | bytes 3168 | tf_op jit(solution)/shard_map/while/body/eval_jaxpr/all_gather | solution.py:44
  1391.7 37.0 %all_gather.110 = bf16[768,3,192]{2,0,1:T(8,128)(2,1)} all-gather(bf16[96,3,192]{2,0,1:T(8,128)(2,1)S(1)} %copy-done.32), channel_id=1, replica_groups=mesh['dp'=8,'mp'=4] {'dp'}, dimensions={0}, use_global_device_ids=true | all-gather | bytes 995328 | tf_op jit(solution)/shard_map/while/body/eval_jaxpr/all_gather | solution.py:36
  1611.3 40.7 %all-gather.21 = bf16[32,24,2]{1,2,0:T(2,128)(2,1)S(1)} all-gather(bf16[1,24,2]{1,2,0:T(2,128)(2,1)} %bitcast.337), channel_id=1, replica_groups=mesh['dp'=8,'mp'=4] {'dp','mp'}, dimensions={0}, use_global_device_ids=true | all-gather | bytes 3168 | tf_op jit(solution)/shard_map/while/body/eval_jaxpr/all_gather | solution.py:44
  1652.4 37.0 %all-gather.20 = bf16[32,24,4]{1,2,0:T(4,128)(2,1)S(1)} all-gather(bf16[1,24,4]{1,2,0:T(4,128)(2,1)} %bitcast.340), channel_id=1, replica_groups=mesh['dp'=8,'mp'=4] {'dp','mp'}, dimensions={0}, use_global_device_ids=true | all-gather | bytes 6336 | tf_op jit(solution)/shard_map/while/body/eval_jaxpr/all_gather | solution.py:45
  1732.9 37.0 %all_gather.99 = bf16[768,3,192]{2,1,0:T(4,128)(2,1)S(1)} all-gather(bf16[96,3,192]{2,1,0:T(4,128)(2,1)S(1)} %copy.86), channel_id=1, replica_groups=mesh['dp'=8,'mp'=4] {'dp'}, dimensions={0}, use_global_device_ids=true | all-gather | bytes 995328 | tf_op jit(solution)/shard_map/while/body/eval_jaxpr/all_gather | solution.py:36
  2072.8 36.6 %all-gather.35.cloned.1.call-done = bf16[768,768]{1,0:T(8,128)(2,1)} async-done(((bf16[96,768]{1,0:T(8,128)(2,1)}), bf16[768,768]{1,0:T(8,128)(2,1)}) %all-gather.35.cloned.1.call-update) | async-done | bytes 1179664 | tf_op jit(solution)/shard_map/while/body/eval_jaxpr/all_gather | solution.py:39
  2118.2 38.9 %all-gather.23 = bf16[32,24,2]{1,2,0:T(2,128)(2,1)S(1)} all-gather(bf16[1,24,2]{1,2,0:T(2,128)(2,1)S(1)} %bitcast.338), channel_id=1, replica_groups=mesh['dp'=8,'mp'=4] {'dp','mp'}, dimensions={0}, use_global_device_ids=true | all-gather | bytes 3168 | tf_op jit(solution)/shard_map/while/body/eval_jaxpr/all_gather | solution.py:44
  2191.0 37.0 %all_gather.110 = bf16[768,3,192]{2,0,1:T(8,128)(2,1)} all-gather(bf16[96,3,192]{2,0,1:T(8,128)(2,1)S(1)} %copy-done.32), channel_id=1, replica_groups=mesh['dp'=8,'mp'=4] {'dp'}, dimensions={0}, use_global_device_ids=true | all-gather | bytes 995328 | tf_op jit(solution)/shard_map/while/body/eval_jaxpr/all_gather | solution.py:36
  2410.6 40.7 %all-gather.21 = bf16[32,24,2]{1,2,0:T(2,128)(2,1)S(1)} all-gather(bf16[1,24,2]{1,2,0:T(2,128)(2,1)} %bitcast.337), channel_id=1, replica_groups=mesh['dp'=8,'mp'=4] {'dp','mp'}, dimensions={0}, use_global_device_ids=true | all-gather | bytes 3168 | tf_op jit(solution)/shard_map/while/body/eval_jaxpr/all_gather | solution.py:44
  2451.6 37.0 %all-gather.20 = bf16[32,24,4]{1,2,0:T(4,128)(2,1)S(1)} all-gather(bf16[1,24,4]{1,2,0:T(4,128)(2,1)} %bitcast.340), channel_id=1, replica_groups=mesh['dp'=8,'mp'=4] {'dp','mp'}, dimensions={0}, use_global_device_ids=true | all-gather | bytes 6336 | tf_op jit(solution)/shard_map/while/body/eval_jaxpr/all_gather | solution.py:45
  2532.2 37.0 %all_gather.99 = bf16[768,3,192]{2,1,0:T(4,128)(2,1)S(1)} all-gather(bf16[96,3,192]{2,1,0:T(4,128)(2,1)S(1)} %copy.86), channel_id=1, replica_groups=mesh['dp'=8,'mp'=4] {'dp'}, dimensions={0}, use_global_device_ids=true | all-gather | bytes 995328 | tf_op jit(solution)/shard_map/while/body/eval_jaxpr/all_gather | solution.py:36
  2872.0 36.6 %all-gather.35.cloned.1.call-done = bf16[768,768]{1,0:T(8,128)(2,1)} async-done(((bf16[96,768]{1,0:T(8,128)(2,1)}), bf16[768,768]{1,0:T(8,128)(2,1)}) %all-gather.35.cloned.1.call-update) | async-done | bytes 1179664 | tf_op jit(solution)/shard_map/while/body/eval_jaxpr/all_gather | solution.py:39
  2917.4 38.9 %all-gather.23 = bf16[32,24,2]{1,2,0:T(2,128)(2,1)S(1)} all-gather(bf16[1,24,2]{1,2,0:T(2,128)(2,1)S(1)} %bitcast.338), channel_id=1, replica_groups=mesh['dp'=8,'mp'=4] {'dp','mp'}, dimensions={0}, use_global_device_ids=true | all-gather | bytes 3168 | tf_op jit(solution)/shard_map/while/body/eval_jaxpr/all_gather | solution.py:44
  2990.2 37.0 %all_gather.110 = bf16[768,3,192]{2,0,1:T(8,128)(2,1)} all-gather(bf16[96,3,192]{2,0,1:T(8,128)(2,1)S(1)} %copy-done.32), channel_id=1, replica_groups=mesh['dp'=8,'mp'=4] {'dp'}, dimensions={0}, use_global_device_ids=true | all-gather | bytes 995328 | tf_op jit(solution)/shard_map/while/body/eval_jaxpr/all_gather | solution.py:36
  3243.7 37.3 %all-reduce.7 = (f32[2,768]{1,0:T(2,128)S(1)}, f32[4,768]{1,0:T(4,128)S(1)}) all-reduce(f32[2,768]{1,0:T(2,128)S(1)} %copy-done.55, f32[4,768]{1,0:T(4,128)S(1)} %copy-done.42), channel_id=13, replica_groups=mesh['dp'=8,'mp'=4] {'dp','mp'}, use_global_device_ids=true, to_apply=%region_38.39.clone | all-reduce | flops 4608 | bytes 36864
  3284.4 56.9 %reduce-scatter.23.cloned.1.call-done = f32[96,192]{1,0:T(8,128)} async-done(((f32[768,192]{1,0:T(8,128)}), f32[96,192]{1,0:T(8,128)}) %reduce-scatter.23.cloned.1.call-update) | async-done | bytes 73744
  3342.9 71.2 %reduce-scatter.17.cloned.1.call-done = f32[96,3,192]{2,0,1:T(8,128)} async-done(((f32[768,3,192]{2,0,1:T(8,128)}), f32[96,3,192]{2,0,1:T(8,128)}) %reduce-scatter.17.cloned.1.call-update) | async-done | bytes 221200 | tf_op jit(solution)/shard_map/reduce_scatter | solution.py:341
  3414.1 72.8 %reduce-scatter.19.cloned.1.call-done = f32[96,768]{1,0:T(8,128)} async-done(((f32[768,768]{1,0:T(8,128)}), f32[96,768]{1,0:T(8,128)}) %reduce-scatter.19.cloned.1.call-update) | async-done | bytes 294928 | tf_op jit(solution)/shard_map/reduce_scatter | solution.py:344
  3486.8 73.1 %reduce-scatter.21.cloned.1.call-done = f32[768,96]{0,1:T(8,128)} async-done(((f32[768,768]{0,1:T(8,128)}), f32[768,96]{0,1:T(8,128)}) %reduce-scatter.21.cloned.1.call-update) | async-done | bytes 294928 | tf_op jit(solution)/shard_map/reduce_scatter | solution.py:346
  (1394 shorter events, 2246.7 us)
Async XLA Ops:
  10.1 330.3 %reduce-scatter.27.cloned.1.call-start = ((), (), s32[]{:S(2)}) async-start(), calls=%async_computation.14 | async-start | bytes 1105920 | tf_op jit(solution)/shard_map/while/body/eval_jaxpr/reduce_scatter | solution.py:64
  177.0 77.0 %collective-permute-start.4 = (bf16[576,2,192]{0,2,1:T(8,128)(2,1)S(1)}, bf16[576,2,192]{0,2,1:T(8,128)(2,1)S(1)}, u32[]{:S(2)}, u32[]{:S(2)}) collective-permute-start(bf16[576,2,192]{0,2,1:T(8,128)(2,1)S(1)} %slice.463), channel_id=1, source_target_pairs={{8,0},{12,4},{16,8},{20,12},{24,16},{28,20},{9,1},{13,5},{17,9},{2... | collective-permute-start | bytes 1327112 | tf_op jit(solution)/shard_map/while/body/eval_jaxpr/ppermute | solution.py:16
  311.8 90.4 %all-gather.31.cloned.1.call-start = ((), (), s32[]{:S(2)}) async-start(), calls=%async_computation.16 | async-start | bytes 1327104 | tf_op jit(solution)/shard_map/while/body/eval_jaxpr/all_gather | solution.py:41
  312.4 115.5 %reduce-scatter.29.cloned.1.call-start = ((), (), s32[]{:S(2)}) async-start(), calls=%async_computation.17 | async-start | bytes 1105920 | tf_op jit(solution)/shard_map/while/body/eval_jaxpr/reduce_scatter | solution.py:64
  429.7 83.5 %all-gather.35.cloned.1.call-start = ((), (), s32[]{:S(2)}) async-start(), calls=%async_computation.19 | async-start | bytes 1327104 | tf_op jit(solution)/shard_map/while/body/eval_jaxpr/all_gather | solution.py:39
  430.4 203.3 %reduce-scatter.31.cloned.1.call-start = ((), (), s32[]{:S(2)}) async-start(), calls=%async_computation.20 | async-start | bytes 1105920 | tf_op jit(solution)/shard_map/while/body/eval_jaxpr/reduce_scatter | solution.py:80
  516.6 288.1 %reduce-scatter.33.cloned.1.call-start = ((), (), s32[]{:S(2)}) async-start(), calls=%async_computation.21 | async-start | bytes 1105920 | tf_op jit(solution)/shard_map/while/body/eval_jaxpr/reduce_scatter | solution.py:80
  809.7 327.2 %reduce-scatter.27.cloned.1.call-start = ((), (), s32[]{:S(2)}) async-start(), calls=%async_computation.14 | async-start | bytes 1105920 | tf_op jit(solution)/shard_map/while/body/eval_jaxpr/reduce_scatter | solution.py:64
  973.9 77.0 %collective-permute-start.4 = (bf16[576,2,192]{0,2,1:T(8,128)(2,1)S(1)}, bf16[576,2,192]{0,2,1:T(8,128)(2,1)S(1)}, u32[]{:S(2)}, u32[]{:S(2)}) collective-permute-start(bf16[576,2,192]{0,2,1:T(8,128)(2,1)S(1)} %slice.463), channel_id=1, source_target_pairs={{8,0},{12,4},{16,8},{20,12},{24,16},{28,20},{9,1},{13,5},{17,9},{2... | collective-permute-start | bytes 1327112 | tf_op jit(solution)/shard_map/while/body/eval_jaxpr/ppermute | solution.py:16
  1108.4 90.8 %all-gather.31.cloned.1.call-start = ((), (), s32[]{:S(2)}) async-start(), calls=%async_computation.16 | async-start | bytes 1327104 | tf_op jit(solution)/shard_map/while/body/eval_jaxpr/all_gather | solution.py:41
  1109.2 115.8 %reduce-scatter.29.cloned.1.call-start = ((), (), s32[]{:S(2)}) async-start(), calls=%async_computation.17 | async-start | bytes 1105920 | tf_op jit(solution)/shard_map/while/body/eval_jaxpr/reduce_scatter | solution.py:64
  1226.7 83.4 %all-gather.35.cloned.1.call-start = ((), (), s32[]{:S(2)}) async-start(), calls=%async_computation.19 | async-start | bytes 1327104 | tf_op jit(solution)/shard_map/while/body/eval_jaxpr/all_gather | solution.py:39
  1227.3 205.7 %reduce-scatter.31.cloned.1.call-start = ((), (), s32[]{:S(2)}) async-start(), calls=%async_computation.20 | async-start | bytes 1105920 | tf_op jit(solution)/shard_map/while/body/eval_jaxpr/reduce_scatter | solution.py:80
  1313.5 290.6 %reduce-scatter.33.cloned.1.call-start = ((), (), s32[]{:S(2)}) async-start(), calls=%async_computation.21 | async-start | bytes 1105920 | tf_op jit(solution)/shard_map/while/body/eval_jaxpr/reduce_scatter | solution.py:80
  1609.0 327.2 %reduce-scatter.27.cloned.1.call-start = ((), (), s32[]{:S(2)}) async-start(), calls=%async_computation.14 | async-start | bytes 1105920 | tf_op jit(solution)/shard_map/while/body/eval_jaxpr/reduce_scatter | solution.py:64
  1773.2 77.0 %collective-permute-start.4 = (bf16[576,2,192]{0,2,1:T(8,128)(2,1)S(1)}, bf16[576,2,192]{0,2,1:T(8,128)(2,1)S(1)}, u32[]{:S(2)}, u32[]{:S(2)}) collective-permute-start(bf16[576,2,192]{0,2,1:T(8,128)(2,1)S(1)} %slice.463), channel_id=1, source_target_pairs={{8,0},{12,4},{16,8},{20,12},{24,16},{28,20},{9,1},{13,5},{17,9},{2... | collective-permute-start | bytes 1327112 | tf_op jit(solution)/shard_map/while/body/eval_jaxpr/ppermute | solution.py:16
  1907.6 90.7 %all-gather.31.cloned.1.call-start = ((), (), s32[]{:S(2)}) async-start(), calls=%async_computation.16 | async-start | bytes 1327104 | tf_op jit(solution)/shard_map/while/body/eval_jaxpr/all_gather | solution.py:41
  1908.4 115.7 %reduce-scatter.29.cloned.1.call-start = ((), (), s32[]{:S(2)}) async-start(), calls=%async_computation.17 | async-start | bytes 1105920 | tf_op jit(solution)/shard_map/while/body/eval_jaxpr/reduce_scatter | solution.py:64
  2025.8 83.5 %all-gather.35.cloned.1.call-start = ((), (), s32[]{:S(2)}) async-start(), calls=%async_computation.19 | async-start | bytes 1327104 | tf_op jit(solution)/shard_map/while/body/eval_jaxpr/all_gather | solution.py:39
  2026.6 205.7 %reduce-scatter.31.cloned.1.call-start = ((), (), s32[]{:S(2)}) async-start(), calls=%async_computation.20 | async-start | bytes 1105920 | tf_op jit(solution)/shard_map/while/body/eval_jaxpr/reduce_scatter | solution.py:80
  2112.7 290.6 %reduce-scatter.33.cloned.1.call-start = ((), (), s32[]{:S(2)}) async-start(), calls=%async_computation.21 | async-start | bytes 1105920 | tf_op jit(solution)/shard_map/while/body/eval_jaxpr/reduce_scatter | solution.py:80
  2408.3 327.2 %reduce-scatter.27.cloned.1.call-start = ((), (), s32[]{:S(2)}) async-start(), calls=%async_computation.14 | async-start | bytes 1105920 | tf_op jit(solution)/shard_map/while/body/eval_jaxpr/reduce_scatter | solution.py:64
  2572.5 77.0 %collective-permute-start.4 = (bf16[576,2,192]{0,2,1:T(8,128)(2,1)S(1)}, bf16[576,2,192]{0,2,1:T(8,128)(2,1)S(1)}, u32[]{:S(2)}, u32[]{:S(2)}) collective-permute-start(bf16[576,2,192]{0,2,1:T(8,128)(2,1)S(1)} %slice.463), channel_id=1, source_target_pairs={{8,0},{12,4},{16,8},{20,12},{24,16},{28,20},{9,1},{13,5},{17,9},{2... | collective-permute-start | bytes 1327112 | tf_op jit(solution)/shard_map/while/body/eval_jaxpr/ppermute | solution.py:16
  2706.9 90.6 %all-gather.31.cloned.1.call-start = ((), (), s32[]{:S(2)}) async-start(), calls=%async_computation.16 | async-start | bytes 1327104 | tf_op jit(solution)/shard_map/while/body/eval_jaxpr/all_gather | solution.py:41
  2707.6 115.6 %reduce-scatter.29.cloned.1.call-start = ((), (), s32[]{:S(2)}) async-start(), calls=%async_computation.17 | async-start | bytes 1105920 | tf_op jit(solution)/shard_map/while/body/eval_jaxpr/reduce_scatter | solution.py:64
  2825.0 83.5 %all-gather.35.cloned.1.call-start = ((), (), s32[]{:S(2)}) async-start(), calls=%async_computation.19 | async-start | bytes 1327104 | tf_op jit(solution)/shard_map/while/body/eval_jaxpr/all_gather | solution.py:39
  2825.8 205.7 %reduce-scatter.31.cloned.1.call-start = ((), (), s32[]{:S(2)}) async-start(), calls=%async_computation.20 | async-start | bytes 1105920 | tf_op jit(solution)/shard_map/while/body/eval_jaxpr/reduce_scatter | solution.py:80
  2911.9 290.6 %reduce-scatter.33.cloned.1.call-start = ((), (), s32[]{:S(2)}) async-start(), calls=%async_computation.21 | async-start | bytes 1105920 | tf_op jit(solution)/shard_map/while/body/eval_jaxpr/reduce_scatter | solution.py:80
  3211.4 129.8 %reduce-scatter.23.cloned.1.call-start = ((), (), s32[]{:S(2)}) async-start(), calls=%async_computation.12 | async-start | bytes 884736
  3213.7 200.3 %reduce-scatter.17.cloned.1.call-start = ((), (), s32[]{:S(2)}) async-start(), calls=%async_computation.9 | async-start | bytes 2654208 | tf_op jit(solution)/shard_map/reduce_scatter | solution.py:341
  3216.8 270.0 %reduce-scatter.19.cloned.1.call-start = ((), (), s32[]{:S(2)}) async-start(), calls=%async_computation.10 | async-start | bytes 2654208 | tf_op jit(solution)/shard_map/reduce_scatter | solution.py:344
  3217.4 342.6 %reduce-scatter.21.cloned.1.call-start = ((), (), s32[]{:S(2)}) async-start(), calls=%async_computation.11 | async-start | bytes 2654208 | tf_op jit(solution)/shard_map/reduce_scatter | solution.py:346
  (366 other events, 9821.8 us)
Sparse Core Ops, SparseCore 0:
  311.3 29.0 reduce-scatter.26
  405.7 22.1 reduce-scatter.28
  516.7 22.1 reduce-scatter.30
  763.5 41.1 reduce-scatter.32
  1107.8 29.0 reduce-scatter.26
  1202.8 22.1 reduce-scatter.28
  1313.6 22.1 reduce-scatter.30
  1562.9 41.1 reduce-scatter.32
  1907.2 29.0 reduce-scatter.26
  2001.9 22.1 reduce-scatter.28
  2112.9 22.1 reduce-scatter.30
  2362.1 41.1 reduce-scatter.32
  2706.4 29.0 reduce-scatter.26
  2801.1 22.1 reduce-scatter.28
  2912.1 22.1 reduce-scatter.30
  3161.3 41.1 reduce-scatter.32
  3213.5 62.2 reduce-scatter.24
  3278.9 62.2 reduce-scatter.22
  3345.3 68.7 reduce-scatter.16
  3418.0 68.8 reduce-scatter.18
  3490.9 68.9 reduce-scatter.20
Sparse Core Ops, SparseCore 1:
  313.9 46.4 all-gather.28
  362.4 39.7 all-gather.30
  429.8 41.4 all-gather.32
  473.4 39.7 all-gather.34
  1110.7 46.4 all-gather.28
  1159.3 39.9 all-gather.30
  1226.8 41.4 all-gather.32
  1270.3 39.7 all-gather.34
  1909.7 46.5 all-gather.28
  1958.5 39.7 all-gather.30
  2025.9 41.4 all-gather.32
  2069.6 39.7 all-gather.34
  2709.0 46.5 all-gather.28
  2757.7 39.7 all-gather.30
  2825.1 41.4 all-gather.32
  2868.8 39.7 all-gather.34
where the time goes:
time: 3580 us; the launch traced here: 3570 us
  blocking collectives  1450 us (41%)
  waiting for transfers between devices  1050 us (29%)
  matrix products  374 us (10%)
  other arithmetic  347 us (10%)
  local copies, waits for them, and re-layouts  193 us (5%)
  starting transfers between devices  122 us (3%)
    all_gather x8, blocking collectives, fetch_weights(): lax.all_gather(gains, ('dp', 'mp'), axis=1, tiled=True)  321 us
    all_gather x8, blocking collectives, fetch_weights(): lax.all_gather(w_qkv, 'dp', axis=0, tiled=True)  296 us
    all_gather x8, blocking collectives, fetch_weights(): lax.all_gather(w_out, 'dp', axis=1, tiled=True)  267 us
    all_gather x8, waiting for transfers between devices, fetch_weights(): lax.all_gather(w_down, 'dp', axis=1, tiled=True)  260 us
    all_gather x8, waiting for transfers between devices, fetch_weights(): lax.all_gather(w_up, 'dp', axis=0, tiled=True)  175 us
    all_gather x4, blocking collectives, fetch_weights(): lax.all_gather(biases, ('dp', 'mp'), axis=1, tiled=True)  148 us
    convert_element_type x12, other arithmetic, backward_pass(): grad_scores = (soft_weights * (grad_soft - row_delta)).astype(jnp.bfloat16)  139 us
    reduce_scatter x8, waiting for transfers between devices, project_back(): lax.psum_scatter(term(jnp.int32(0), share_rows * lax.axis_size('mp')).ast...  135 us
  transfers between devices with their start and end apart: 85, of which 52 were waited for; matrix products, arithmetic and copies ran while one was open for 8% of the time, Pallas kernels for 0%

commit v1 on v0

--- a/solution.py
+++ b/solution.py
@@ -8,6 +8,28 @@
 CLIP = 1500
 epsilon = 1e-05
 masked_score = -1e30
+
+
+def joined_along(pieces, dim):
+    pieces = jnp.moveaxis(pieces, 0, dim)
+    lengths = pieces.shape
+    return pieces.reshape(*lengths[:dim], lengths[dim] * lengths[dim + 1], *lengths[dim + 2 :])
+
+
+def ring_gather(x, axis, dim):
+    size = lax.axis_size(axis)
+    pairs = [(i, (i + 1) % size) for i in range(size)]
+    back = [(b, a) for a, b in pairs]
+    lower, upper = ([], [])
+    for step in range(size - 1):
+        if step % 2 == 0:
+            lower.append(lax.ppermute(lower[-1] if lower else x, axis, pairs))
+        else:
+            upper.append(lax.ppermute(upper[-1] if upper else x, axis, back))
+    parts = jnp.stack([*lower[::-1], x, *upper])
+    shift = lax.axis_index(axis) - len(lower)
+    parts = parts[(jnp.arange(size) - shift) % size]
+    return joined_along(parts, dim)
 
 
 def passed_along(array, axis, by):
@@ -38,7 +60,7 @@
         lax.all_gather(w_out, "dp", axis=1, tiled=True),
         lax.all_gather(w_up, "dp", axis=0, tiled=True),
         lax.all_gather(b_up, "dp", axis=1, tiled=True),
-        lax.all_gather(w_down, "dp", axis=1, tiled=True),
+        ring_gather(w_down, "dp", 1),
     )
     norm_rows = (
         lax.all_gather(gains, ("dp", "mp"), axis=1, tiled=True),

time: 3580 us -> 3420 us (0.955)
  waiting for transfers between devices: 1050 us -> 792 us
  starting transfers between devices: 122 us -> 204 us
  local copies, waits for them, and re-layouts: 193 us -> 242 us
    all_gather x8 -> x0, waiting for transfers between devices: 260 us -> none  [fetch_weights(): lax.all_gather(w_down, 'dp', axis=1, tiled=True)]
    ppermute x0 -> x35, starting transfers between devices: none -> 82.8 us  [the longest x15 65.6 us: ring_gather(): upper.append(lax.ppermute(upper[-1] if upper else x, axis, back))]
    ppermute x0 -> x35, waiting for transfers between devices: none -> 63.2 us  [the longest x20 62.3 us: ring_gather(): lower.append(lax.ppermute(lower[-1] if lower else x, axis, pairs))]
    all_gather x8, waiting for transfers between devices: 175 us -> 118 us  [fetch_weights(): lax.all_gather(w_up, 'dp', axis=0, tiled=True)]
  transfers between devices with their start and end apart: 85 -> 112, of which waited for: 52 -> 62; matrix products, arithmetic and copies ran while one was open for 8% -> 9% of each run, Pallas kernels for 0% -> 0%
where the time goes in v1:
time: 3420 us; the launch traced here: 3410 us
  blocking collectives  1440 us (42%)
  waiting for transfers between devices  792 us (23%)
  matrix products  366 us (11%)
  other arithmetic  338 us (10%)
  local copies, waits for them, and re-layouts  242 us (7%)
  starting transfers between devices  204 us (6%)
    all_gather x8, blocking collectives, fetch_weights(): lax.all_gather(gains, ('dp', 'mp'), axis=1, tiled=True)  320 us
    all_gather x8, blocking collectives, fetch_weights(): lax.all_gather(w_qkv, 'dp', axis=0, tiled=True)  295 us
    all_gather x8, blocking collectives, fetch_weights(): lax.all_gather(w_out, 'dp', axis=1, tiled=True)  268 us
    all_gather x4, blocking collectives, fetch_weights(): lax.all_gather(biases, ('dp', 'mp'), axis=1, tiled=True)  148 us
    convert_element_type x12, other arithmetic, backward_pass(): grad_scores = (soft_weights * (grad_soft - row_delta)).astype(jnp.bfloat16)  138 us
    reduce_scatter x8, waiting for transfers between devices, project_back(): lax.psum_scatter(term(jnp.int32(0), share_rows * lax.axis_size('mp')).ast...  136 us
    all_gather x4, blocking collectives, fetch_weights(): lax.all_gather(b_qv, 'dp', axis=2, tiled=True)  122 us
    ppermute x48, starting transfers between devices, passed_along(): return lax.ppermute(array, axis, pairs)  120 us
  transfers between devices with their start and end apart: 112, of which 62 were waited for; matrix products, arithmetic and copies ran while one was open for 9% of the time, Pallas kernels for 0%

profile of v1, /device:TPU:0, one launch (start us, length us, event | category | flops | bytes accessed | tf_op | source)
XLA Modules:
  0.0 3411.4 jit_solution(8095684431699449687)
XLA Ops:
  44.7 3008.8 %while.33 = (s32[]{:T(128)}, f32[768,3,192]{0,2,1:T(8,128)}, f32[2,1,192]{2,1,0:T(1,128)}, f32[192,768]{1,0:T(8,128)}, f32[768,768]{1,0:T(8,128)}, /*index=5*/f3...) while((s32[]{:T(128)}, f32[768,3,192]{0,2,1:T(8,128)}, ...), condition=%wide.region_31.32_spmd.clone.clone.clone, body=%wide.region_0.31_spmd.clone.clone.clone.sunk | while | flops 11638807552 | bytes 784896000 | solution.py:361
  45.4 42.4 %all-gather.21 = bf16[32,24,2]{1,2,0:T(2,128)(2,1)S(1)} all-gather(bf16[1,24,2]{1,2,0:T(2,128)(2,1)S(1)} %bitcast.404), channel_id=1, replica_groups=mesh['dp'=8,'mp'=4] {'dp','mp'}, dimensions={0}, use_global_device_ids=true | all-gather | bytes 3168 | tf_op jit(solution)/shard_map/while/body/eval_jaxpr/all_gather | solution.py:66
  88.1 37.0 %all-gather.20 = bf16[32,24,4]{1,2,0:T(4,128)(2,1)S(1)} all-gather(bf16[1,24,4]{1,2,0:T(4,128)(2,1)} %bitcast.354), channel_id=1, replica_groups=mesh['dp'=8,'mp'=4] {'dp','mp'}, dimensions={0}, use_global_device_ids=true | all-gather | bytes 6336 | tf_op jit(solution)/shard_map/while/body/eval_jaxpr/all_gather | solution.py:67
  166.8 37.0 %all_gather.130 = bf16[768,3,192]{2,1,0:T(4,128)(2,1)S(1)} all-gather(bf16[96,3,192]{2,1,0:T(4,128)(2,1)S(1)} %copy.98), channel_id=1, replica_groups=mesh['dp'=8,'mp'=4] {'dp'}, dimensions={0}, use_global_device_ids=true | all-gather | bytes 995328 | tf_op jit(solution)/shard_map/while/body/eval_jaxpr/all_gather | solution.py:58
  247.1 33.4 all_gather.133
  509.0 39.1 %all-gather.23 = bf16[32,24,2]{1,2,0:T(2,128)(2,1)S(1)} all-gather(bf16[1,24,2]{1,2,0:T(2,128)(2,1)} %bitcast.403), channel_id=1, replica_groups=mesh['dp'=8,'mp'=4] {'dp','mp'}, dimensions={0}, use_global_device_ids=true | all-gather | bytes 3168 | tf_op jit(solution)/shard_map/while/body/eval_jaxpr/all_gather | solution.py:66
  548.4 33.5 all_gather.138
  581.9 36.8 %all_gather.139 = bf16[768,3,192]{2,0,1:T(8,128)(2,1)} all-gather(bf16[96,3,192]{2,0,1:T(8,128)(2,1)} %get-tuple-element.1252), channel_id=1, replica_groups=mesh['dp'=8,'mp'=4] {'dp'}, dimensions={0}, use_global_device_ids=true | all-gather | bytes 995328 | tf_op jit(solution)/shard_map/while/body/eval_jaxpr/all_gather | solution.py:58
  755.5 36.0 %reduce-scatter.33.cloned.1.call-done = bf16[144,768]{1,0:T(8,128)(2,1)} async-done(((bf16[576,768]{1,0:T(8,128)(2,1)}), bf16[144,768]{1,0:T(8,128)(2,1)}) %reduce-scatter.33.cloned.1.call-update) | async-done | bytes 221200 | tf_op jit(solution)/shard_map/while/body/eval_jaxpr/reduce_scatter | solution.py:102
  796.6 40.6 %all-gather.21 = bf16[32,24,2]{1,2,0:T(2,128)(2,1)S(1)} all-gather(bf16[1,24,2]{1,2,0:T(2,128)(2,1)S(1)} %bitcast.404), channel_id=1, replica_groups=mesh['dp'=8,'mp'=4] {'dp','mp'}, dimensions={0}, use_global_device_ids=true | all-gather | bytes 3168 | tf_op jit(solution)/shard_map/while/body/eval_jaxpr/all_gather | solution.py:66
  837.4 37.0 %all-gather.20 = bf16[32,24,4]{1,2,0:T(4,128)(2,1)S(1)} all-gather(bf16[1,24,4]{1,2,0:T(4,128)(2,1)} %bitcast.354), channel_id=1, replica_groups=mesh['dp'=8,'mp'=4] {'dp','mp'}, dimensions={0}, use_global_device_ids=true | all-gather | bytes 6336 | tf_op jit(solution)/shard_map/while/body/eval_jaxpr/all_gather | solution.py:67
  916.1 37.0 %all_gather.130 = bf16[768,3,192]{2,1,0:T(4,128)(2,1)S(1)} all-gather(bf16[96,3,192]{2,1,0:T(4,128)(2,1)S(1)} %copy.98), channel_id=1, replica_groups=mesh['dp'=8,'mp'=4] {'dp'}, dimensions={0}, use_global_device_ids=true | all-gather | bytes 995328 | tf_op jit(solution)/shard_map/while/body/eval_jaxpr/all_gather | solution.py:58
  1258.8 39.1 %all-gather.23 = bf16[32,24,2]{1,2,0:T(2,128)(2,1)S(1)} all-gather(bf16[1,24,2]{1,2,0:T(2,128)(2,1)} %bitcast.403), channel_id=1, replica_groups=mesh['dp'=8,'mp'=4] {'dp','mp'}, dimensions={0}, use_global_device_ids=true | all-gather | bytes 3168 | tf_op jit(solution)/shard_map/while/body/eval_jaxpr/all_gather | solution.py:66
  1298.2 33.5 all_gather.138
  1331.7 36.8 %all_gather.139 = bf16[768,3,192]{2,0,1:T(8,128)(2,1)} all-gather(bf16[96,3,192]{2,0,1:T(8,128)(2,1)} %get-tuple-element.1252), channel_id=1, replica_groups=mesh['dp'=8,'mp'=4] {'dp'}, dimensions={0}, use_global_device_ids=true | all-gather | bytes 995328 | tf_op jit(solution)/shard_map/while/body/eval_jaxpr/all_gather | solution.py:58
  1548.2 40.6 %all-gather.21 = bf16[32,24,2]{1,2,0:T(2,128)(2,1)S(1)} all-gather(bf16[1,24,2]{1,2,0:T(2,128)(2,1)S(1)} %bitcast.404), channel_id=1, replica_groups=mesh['dp'=8,'mp'=4] {'dp','mp'}, dimensions={0}, use_global_device_ids=true | all-gather | bytes 3168 | tf_op jit(solution)/shard_map/while/body/eval_jaxpr/all_gather | solution.py:66
  1589.0 37.0 %all-gather.20 = bf16[32,24,4]{1,2,0:T(4,128)(2,1)S(1)} all-gather(bf16[1,24,4]{1,2,0:T(4,128)(2,1)} %bitcast.354), channel_id=1, replica_groups=mesh['dp'=8,'mp'=4] {'dp','mp'}, dimensions={0}, use_global_device_ids=true | all-gather | bytes 6336 | tf_op jit(solution)/shard_map/while/body/eval_jaxpr/all_gather | solution.py:67
  1667.7 37.0 %all_gather.130 = bf16[768,3,192]{2,1,0:T(4,128)(2,1)S(1)} all-gather(bf16[96,3,192]{2,1,0:T(4,128)(2,1)S(1)} %copy.98), channel_id=1, replica_groups=mesh['dp'=8,'mp'=4] {'dp'}, dimensions={0}, use_global_device_ids=true | all-gather | bytes 995328 | tf_op jit(solution)/shard_map/while/body/eval_jaxpr/all_gather | solution.py:58
  2010.7 39.1 %all-gather.23 = bf16[32,24,2]{1,2,0:T(2,128)(2,1)S(1)} all-gather(bf16[1,24,2]{1,2,0:T(2,128)(2,1)} %bitcast.403), channel_id=1, replica_groups=mesh['dp'=8,'mp'=4] {'dp','mp'}, dimensions={0}, use_global_device_ids=true | all-gather | bytes 3168 | tf_op jit(solution)/shard_map/while/body/eval_jaxpr/all_gather | solution.py:66
  2050.0 33.5 all_gather.138
  2083.5 36.8 %all_gather.139 = bf16[768,3,192]{2,0,1:T(8,128)(2,1)} all-gather(bf16[96,3,192]{2,0,1:T(8,128)(2,1)} %get-tuple-element.1252), channel_id=1, replica_groups=mesh['dp'=8,'mp'=4] {'dp'}, dimensions={0}, use_global_device_ids=true | all-gather | bytes 995328 | tf_op jit(solution)/shard_map/while/body/eval_jaxpr/all_gather | solution.py:58
  2300.0 40.6 %all-gather.21 = bf16[32,24,2]{1,2,0:T(2,128)(2,1)S(1)} all-gather(bf16[1,24,2]{1,2,0:T(2,128)(2,1)S(1)} %bitcast.404), channel_id=1, replica_groups=mesh['dp'=8,'mp'=4] {'dp','mp'}, dimensions={0}, use_global_device_ids=true | all-gather | bytes 3168 | tf_op jit(solution)/shard_map/while/body/eval_jaxpr/all_gather | solution.py:66
  2340.8 37.0 %all-gather.20 = bf16[32,24,4]{1,2,0:T(4,128)(2,1)S(1)} all-gather(bf16[1,24,4]{1,2,0:T(4,128)(2,1)} %bitcast.354), channel_id=1, replica_groups=mesh['dp'=8,'mp'=4] {'dp','mp'}, dimensions={0}, use_global_device_ids=true | all-gather | bytes 6336 | tf_op jit(solution)/shard_map/while/body/eval_jaxpr/all_gather | solution.py:67
  2419.5 37.0 %all_gather.130 = bf16[768,3,192]{2,1,0:T(4,128)(2,1)S(1)} all-gather(bf16[96,3,192]{2,1,0:T(4,128)(2,1)S(1)} %copy.98), channel_id=1, replica_groups=mesh['dp'=8,'mp'=4] {'dp'}, dimensions={0}, use_global_device_ids=true | all-gather | bytes 995328 | tf_op jit(solution)/shard_map/while/body/eval_jaxpr/all_gather | solution.py:58
  2762.2 39.1 %all-gather.23 = bf16[32,24,2]{1,2,0:T(2,128)(2,1)S(1)} all-gather(bf16[1,24,2]{1,2,0:T(2,128)(2,1)} %bitcast.403), channel_id=1, replica_groups=mesh['dp'=8,'mp'=4] {'dp','mp'}, dimensions={0}, use_global_device_ids=true | all-gather | bytes 3168 | tf_op jit(solution)/shard_map/while/body/eval_jaxpr/all_gather | solution.py:66
  2801.6 33.5 all_gather.138
  2835.1 36.8 %all_gather.139 = bf16[768,3,192]{2,0,1:T(8,128)(2,1)} all-gather(bf16[96,3,192]{2,0,1:T(8,128)(2,1)} %get-tuple-element.1252), channel_id=1, replica_groups=mesh['dp'=8,'mp'=4] {'dp'}, dimensions={0}, use_global_device_ids=true | all-gather | bytes 995328 | tf_op jit(solution)/shard_map/while/body/eval_jaxpr/all_gather | solution.py:58
  3087.6 37.3 %all-reduce.7 = (f32[2,768]{1,0:T(2,128)S(1)}, f32[4,768]{1,0:T(4,128)S(1)}) all-reduce(f32[2,768]{1,0:T(2,128)S(1)} %copy-done.53, f32[4,768]{1,0:T(4,128)S(1)} %copy-done.42), channel_id=13, replica_groups=mesh['dp'=8,'mp'=4] {'dp','mp'}, use_global_device_ids=true, to_apply=%region_38.39.clone | all-reduce | flops 4608 | bytes 36864
  3128.3 57.0 %reduce-scatter.23.cloned.1.call-done = f32[96,192]{1,0:T(8,128)} async-done(((f32[768,192]{1,0:T(8,128)}), f32[96,192]{1,0:T(8,128)}) %reduce-scatter.23.cloned.1.call-update) | async-done | bytes 73744
  3186.9 71.1 %reduce-scatter.17.cloned.1.call-done = f32[96,3,192]{2,0,1:T(8,128)} async-done(((f32[768,3,192]{2,0,1:T(8,128)}), f32[96,3,192]{2,0,1:T(8,128)}) %reduce-scatter.17.cloned.1.call-update) | async-done | bytes 221200 | tf_op jit(solution)/shard_map/reduce_scatter | solution.py:363
  3258.0 72.9 %reduce-scatter.19.cloned.1.call-done = f32[96,768]{1,0:T(8,128)} async-done(((f32[768,768]{1,0:T(8,128)}), f32[96,768]{1,0:T(8,128)}) %reduce-scatter.19.cloned.1.call-update) | async-done | bytes 294928 | tf_op jit(solution)/shard_map/reduce_scatter | solution.py:366
  3330.9 72.9 %reduce-scatter.21.cloned.1.call-done = f32[768,96]{0,1:T(8,128)} async-done(((f32[768,768]{0,1:T(8,128)}), f32[768,96]{0,1:T(8,128)}) %reduce-scatter.21.cloned.1.call-update) | async-done | bytes 294928 | tf_op jit(solution)/shard_map/reduce_scatter | solution.py:368
  (1462 shorter events, 2104.8 us)
Async XLA Ops:
  45.0 326.4 %reduce-scatter.27.cloned.1.call-start = ((), (), s32[]{:S(2)}) async-start(), calls=%async_computation.14 | async-start | bytes 1105920 | tf_op jit(solution)/shard_map/while/body/eval_jaxpr/reduce_scatter | solution.py:86
  207.1 77.2 %collective-permute-start.4 = (bf16[576,2,192]{0,2,1:T(8,128)(2,1)S(1)}, bf16[576,2,192]{0,2,1:T(8,128)(2,1)S(1)}, u32[]{:S(2)}, u32[]{:S(2)}) collective-permute-start(bf16[576,2,192]{0,2,1:T(8,128)(2,1)S(1)} %slice.574), channel_id=1, source_target_pairs={{8,0},{12,4},{16,8},{20,12},{24,16},{28,20},{9,1},{13,5},{17,9},{2... | collective-permute-start | bytes 1327112 | tf_op jit(solution)/shard_map/while/body/eval_jaxpr/ppermute | solution.py:38
  208.4 75.9 %collective-permute-start.3 = (bf16[576,2,192]{0,2,1:T(8,128)(2,1)S(1)}, bf16[576,2,192]{0,2,1:T(8,128)(2,1)S(1)}, u32[]{:S(2)}, u32[]{:S(2)}) collective-permute-start(bf16[576,2,192]{0,2,1:T(8,128)(2,1)S(1)} %slice.574), channel_id=1, source_target_pairs={{4,0},{8,4},{12,8},{16,12},{20,16},{24,20},{28,24},{5,1},{9,5},{13... | collective-permute-start | bytes 1327112 | tf_op jit(solution)/shard_map/while/body/eval_jaxpr/ppermute | solution.py:38
  342.8 80.8 %reduce-scatter.29.cloned.1.call-start = ((), (), s32[]{:S(2)}) async-start(), calls=%async_computation.16 | async-start | bytes 1105920 | tf_op jit(solution)/shard_map/while/body/eval_jaxpr/reduce_scatter | solution.py:86
  401.3 99.8 %all-gather.29.cloned.1.call-start = ((), (), s32[]{:S(2)}) async-start(), calls=%async_computation.17 | async-start | bytes 1327104 | tf_op jit(solution)/shard_map/while/body/eval_jaxpr/all_gather | solution.py:61
  458.8 162.6 %reduce-scatter.31.cloned.1.call-start = ((), (), s32[]{:S(2)}) async-start(), calls=%async_computation.18 | async-start | bytes 1105920 | tf_op jit(solution)/shard_map/while/body/eval_jaxpr/reduce_scatter | solution.py:102
  504.4 287.1 %reduce-scatter.33.cloned.1.call-start = ((), (), s32[]{:S(2)}) async-start(), calls=%async_computation.19 | async-start | bytes 1105920 | tf_op jit(solution)/shard_map/while/body/eval_jaxpr/reduce_scatter | solution.py:102
  796.2 324.3 %reduce-scatter.27.cloned.1.call-start = ((), (), s32[]{:S(2)}) async-start(), calls=%async_computation.14 | async-start | bytes 1105920 | tf_op jit(solution)/shard_map/while/body/eval_jaxpr/reduce_scatter | solution.py:86
  956.4 77.2 %collective-permute-start.4 = (bf16[576,2,192]{0,2,1:T(8,128)(2,1)S(1)}, bf16[576,2,192]{0,2,1:T(8,128)(2,1)S(1)}, u32[]{:S(2)}, u32[]{:S(2)}) collective-permute-start(bf16[576,2,192]{0,2,1:T(8,128)(2,1)S(1)} %slice.574), channel_id=1, source_target_pairs={{8,0},{12,4},{16,8},{20,12},{24,16},{28,20},{9,1},{13,5},{17,9},{2... | collective-permute-start | bytes 1327112 | tf_op jit(solution)/shard_map/while/body/eval_jaxpr/ppermute | solution.py:38
  957.7 75.9 %collective-permute-start.3 = (bf16[576,2,192]{0,2,1:T(8,128)(2,1)S(1)}, bf16[576,2,192]{0,2,1:T(8,128)(2,1)S(1)}, u32[]{:S(2)}, u32[]{:S(2)}) collective-permute-start(bf16[576,2,192]{0,2,1:T(8,128)(2,1)S(1)} %slice.574), channel_id=1, source_target_pairs={{4,0},{8,4},{12,8},{16,12},{20,16},{24,20},{28,24},{5,1},{9,5},{13... | collective-permute-start | bytes 1327112 | tf_op jit(solution)/shard_map/while/body/eval_jaxpr/ppermute | solution.py:38
  1091.8 80.8 %reduce-scatter.29.cloned.1.call-start = ((), (), s32[]{:S(2)}) async-start(), calls=%async_computation.16 | async-start | bytes 1105920 | tf_op jit(solution)/shard_map/while/body/eval_jaxpr/reduce_scatter | solution.py:86
  1150.3 99.8 %all-gather.29.cloned.1.call-start = ((), (), s32[]{:S(2)}) async-start(), calls=%async_computation.17 | async-start | bytes 1327104 | tf_op jit(solution)/shard_map/while/body/eval_jaxpr/all_gather | solution.py:61
  1207.8 165.1 %reduce-scatter.31.cloned.1.call-start = ((), (), s32[]{:S(2)}) async-start(), calls=%async_computation.18 | async-start | bytes 1105920 | tf_op jit(solution)/shard_map/while/body/eval_jaxpr/reduce_scatter | solution.py:102
  1253.4 289.6 %reduce-scatter.33.cloned.1.call-start = ((), (), s32[]{:S(2)}) async-start(), calls=%async_computation.19 | async-start | bytes 1105920 | tf_op jit(solution)/shard_map/while/body/eval_jaxpr/reduce_scatter | solution.py:102
  1547.7 324.3 %reduce-scatter.27.cloned.1.call-start = ((), (), s32[]{:S(2)}) async-start(), calls=%async_computation.14 | async-start | bytes 1105920 | tf_op jit(solution)/shard_map/while/body/eval_jaxpr/reduce_scatter | solution.py:86
  1708.0 77.2 %collective-permute-start.4 = (bf16[576,2,192]{0,2,1:T(8,128)(2,1)S(1)}, bf16[576,2,192]{0,2,1:T(8,128)(2,1)S(1)}, u32[]{:S(2)}, u32[]{:S(2)}) collective-permute-start(bf16[576,2,192]{0,2,1:T(8,128)(2,1)S(1)} %slice.574), channel_id=1, source_target_pairs={{8,0},{12,4},{16,8},{20,12},{24,16},{28,20},{9,1},{13,5},{17,9},{2... | collective-permute-start | bytes 1327112 | tf_op jit(solution)/shard_map/while/body/eval_jaxpr/ppermute | solution.py:38
  1709.3 75.9 %collective-permute-start.3 = (bf16[576,2,192]{0,2,1:T(8,128)(2,1)S(1)}, bf16[576,2,192]{0,2,1:T(8,128)(2,1)S(1)}, u32[]{:S(2)}, u32[]{:S(2)}) collective-permute-start(bf16[576,2,192]{0,2,1:T(8,128)(2,1)S(1)} %slice.574), channel_id=1, source_target_pairs={{4,0},{8,4},{12,8},{16,12},{20,16},{24,20},{28,24},{5,1},{9,5},{13... | collective-permute-start | bytes 1327112 | tf_op jit(solution)/shard_map/while/body/eval_jaxpr/ppermute | solution.py:38
  1843.5 80.9 %reduce-scatter.29.cloned.1.call-start = ((), (), s32[]{:S(2)}) async-start(), calls=%async_computation.16 | async-start | bytes 1105920 | tf_op jit(solution)/shard_map/while/body/eval_jaxpr/reduce_scatter | solution.py:86
  1902.2 99.8 %all-gather.29.cloned.1.call-start = ((), (), s32[]{:S(2)}) async-start(), calls=%async_computation.17 | async-start | bytes 1327104 | tf_op jit(solution)/shard_map/while/body/eval_jaxpr/all_gather | solution.py:61
  1959.6 165.1 %reduce-scatter.31.cloned.1.call-start = ((), (), s32[]{:S(2)}) async-start(), calls=%async_computation.18 | async-start | bytes 1105920 | tf_op jit(solution)/shard_map/while/body/eval_jaxpr/reduce_scatter | solution.py:102
  2005.3 289.6 %reduce-scatter.33.cloned.1.call-start = ((), (), s32[]{:S(2)}) async-start(), calls=%async_computation.19 | async-start | bytes 1105920 | tf_op jit(solution)/shard_map/while/body/eval_jaxpr/reduce_scatter | solution.py:102
  2299.6 324.3 %reduce-scatter.27.cloned.1.call-start = ((), (), s32[]{:S(2)}) async-start(), calls=%async_computation.14 | async-start | bytes 1105920 | tf_op jit(solution)/shard_map/while/body/eval_jaxpr/reduce_scatter | solution.py:86
  2459.8 77.2 %collective-permute-start.4 = (bf16[576,2,192]{0,2,1:T(8,128)(2,1)S(1)}, bf16[576,2,192]{0,2,1:T(8,128)(2,1)S(1)}, u32[]{:S(2)}, u32[]{:S(2)}) collective-permute-start(bf16[576,2,192]{0,2,1:T(8,128)(2,1)S(1)} %slice.574), channel_id=1, source_target_pairs={{8,0},{12,4},{16,8},{20,12},{24,16},{28,20},{9,1},{13,5},{17,9},{2... | collective-permute-start | bytes 1327112 | tf_op jit(solution)/shard_map/while/body/eval_jaxpr/ppermute | solution.py:38
  2461.1 75.9 %collective-permute-start.3 = (bf16[576,2,192]{0,2,1:T(8,128)(2,1)S(1)}, bf16[576,2,192]{0,2,1:T(8,128)(2,1)S(1)}, u32[]{:S(2)}, u32[]{:S(2)}) collective-permute-start(bf16[576,2,192]{0,2,1:T(8,128)(2,1)S(1)} %slice.574), channel_id=1, source_target_pairs={{4,0},{8,4},{12,8},{16,12},{20,16},{24,20},{28,24},{5,1},{9,5},{13... | collective-permute-start | bytes 1327112 | tf_op jit(solution)/shard_map/while/body/eval_jaxpr/ppermute | solution.py:38
  2595.2 80.8 %reduce-scatter.29.cloned.1.call-start = ((), (), s32[]{:S(2)}) async-start(), calls=%async_computation.16 | async-start | bytes 1105920 | tf_op jit(solution)/shard_map/while/body/eval_jaxpr/reduce_scatter | solution.py:86
  2653.6 99.8 %all-gather.29.cloned.1.call-start = ((), (), s32[]{:S(2)}) async-start(), calls=%async_computation.17 | async-start | bytes 1327104 | tf_op jit(solution)/shard_map/while/body/eval_jaxpr/all_gather | solution.py:61
  2712.0 164.2 %reduce-scatter.31.cloned.1.call-start = ((), (), s32[]{:S(2)}) async-start(), calls=%async_computation.18 | async-start | bytes 1105920 | tf_op jit(solution)/shard_map/while/body/eval_jaxpr/reduce_scatter | solution.py:102
  2756.8 289.6 %reduce-scatter.33.cloned.1.call-start = ((), (), s32[]{:S(2)}) async-start(), calls=%async_computation.19 | async-start | bytes 1105920 | tf_op jit(solution)/shard_map/while/body/eval_jaxpr/reduce_scatter | solution.py:102
  3055.3 130.0 %reduce-scatter.23.cloned.1.call-start = ((), (), s32[]{:S(2)}) async-start(), calls=%async_computation.12 | async-start | bytes 884736
  3057.6 200.4 %reduce-scatter.17.cloned.1.call-start = ((), (), s32[]{:S(2)}) async-start(), calls=%async_computation.9 | async-start | bytes 2654208 | tf_op jit(solution)/shard_map/reduce_scatter | solution.py:363
  3060.7 270.3 %reduce-scatter.19.cloned.1.call-start = ((), (), s32[]{:S(2)}) async-start(), calls=%async_computation.10 | async-start | bytes 2654208 | tf_op jit(solution)/shard_map/reduce_scatter | solution.py:366
  3061.4 342.4 %reduce-scatter.21.cloned.1.call-start = ((), (), s32[]{:S(2)}) async-start(), calls=%async_computation.11 | async-start | bytes 2654208 | tf_op jit(solution)/shard_map/reduce_scatter | solution.py:368
  (378 other events, 7596.0 us)
Sparse Core Ops, SparseCore 0:
  342.4 29.0 reduce-scatter.26
  401.4 22.1 reduce-scatter.28
  504.5 22.1 reduce-scatter.30
  750.3 41.1 reduce-scatter.32
  1091.4 29.0 reduce-scatter.26
  1150.4 22.1 reduce-scatter.28
  1253.6 22.1 reduce-scatter.30
  1501.8 41.1 reduce-scatter.32
  1842.9 29.0 reduce-scatter.26
  1902.3 22.1 reduce-scatter.28
  2005.4 22.1 reduce-scatter.30
  2253.7 41.1 reduce-scatter.32
  2594.8 29.0 reduce-scatter.26
  2653.8 22.1 reduce-scatter.28
  2756.9 22.1 reduce-scatter.30
  3005.2 41.1 reduce-scatter.32
Sparse Core Ops, SparseCore 1:
  344.9 46.6 all-gather.26
  458.8 42.1 all-gather.28
  1093.9 46.6 all-gather.26
  1207.9 42.1 all-gather.28
  1845.8 46.6 all-gather.26
  1959.7 42.1 all-gather.28
  2597.3 46.6 all-gather.26
  2712.1 41.3 all-gather.28
  3057.3 62.3 reduce-scatter.24
  3123.0 62.3 reduce-scatter.22
  3189.2 68.7 reduce-scatter.16
  3262.1 68.8 reduce-scatter.18
  3334.9 68.9 reduce-scatter.20
